TPU v7x, 32 devices: a whole 2x2x4 slice. The times are simulated.
32 devices in a mesh: row: 8 (over z, y), col: 4 (over x, core).
Axes of the slice: x: 2, y: 2, z: 4, core: 2. Of those that a mesh axis runs over, the one named last changes fastest.
Arguments:
- amplitudes: float32 [64, 2, 640], P('row', None, 'col'), may hold values from -6 to 6
- integrals: float32 [2, 640, 640, 640], P(None, 'col', 'row'), may hold values from -0.5 to 0.5
- virt_irrep: int32 [640], replicated, may hold values from 0 to 7
- pair_irrep: int32 [64], replicated, may hold values from 0 to 7
- tile_mask: int32 [8, 8], replicated, may hold values 0 or 1
Outputs:
- residual: float32 [64, 640, 640], P('col', 'row')
All inputs are finite; a program needn't handle non-finite values.
Results may differ from a plain program's by a relative error of at most 0.000071.
Values sent between devices are 32-bit elements; how exact they have to be, the bound alone decides.
A program may use at most 192 MiB of HBM per device.

v0:
```python
import jax
import jax.numpy as jnp
from jax import lax
from jax.sharding import PartitionSpec as P


def reduce_pairs(partial_sums):
    return lax.psum_scatter(partial_sums, "col", scatter_dimension=0, tiled=True)


def mirror_after(owned):
    swapped = lax.all_to_all(owned, "row", split_axis=2, concat_axis=1, tiled=True)
    return owned - jnp.transpose(swapped, (0, 2, 1))


def mask_slab(amps, c_labels, d_labels, pair_irrep, tile_mask):
    labels_range = jnp.arange(tile_mask.shape[0], dtype=jnp.int32)
    c_onehot = (c_labels[:, None] == labels_range[None, :]).astype(jnp.float32)
    d_onehot = (d_labels[:, None] == labels_range[None, :]).astype(jnp.float32)
    tile_float = tile_mask.astype(jnp.float32)
    screen = jnp.dot(
        jnp.dot(
            c_onehot,
            tile_float,
            precision=lax.Precision.HIGHEST,
            preferred_element_type=jnp.float32,
        ),
        d_onehot.T,
        precision=lax.Precision.HIGHEST,
        preferred_element_type=jnp.float32,
    )
    allowed = (
        jnp.bitwise_xor(c_labels[:, None], d_labels[None, :])[None, :, :]
        == pair_irrep[:, None, None]
    )
    return amps * screen[None, :, :] * allowed.astype(jnp.float32)


def local(amplitudes, integrals, virt_irrep, pair_irrep, tile_mask):
    slab_width = amplitudes.shape[1]
    d_width = integrals.shape[1]
    a_width = integrals.shape[2]
    full_width = integrals.shape[3]
    row_index = lax.axis_index("row")
    col_index = lax.axis_index("col")
    gathered = lax.all_gather(amplitudes, "row", axis=0, tiled=True)
    pair_count = gathered.shape[0]
    c_labels = virt_irrep[:slab_width]
    d_labels = lax.dynamic_slice_in_dim(virt_irrep, col_index * d_width, d_width)
    masked = mask_slab(gathered, c_labels, d_labels, pair_irrep, tile_mask)
    partial_sums = jnp.dot(
        masked.reshape(pair_count, slab_width * d_width),
        integrals.reshape(slab_width * d_width, a_width * full_width),
        precision=lax.Precision.HIGHEST,
        preferred_element_type=jnp.float32,
    ).reshape(pair_count, a_width, full_width)
    mirrored = mirror_after(reduce_pairs(partial_sums))
    own_pairs = mirrored.shape[0]
    a_labels = lax.dynamic_slice_in_dim(virt_irrep, row_index * a_width, a_width)
    pair_labels = lax.dynamic_slice_in_dim(pair_irrep, col_index * own_pairs, own_pairs)
    kept_mask = (
        jnp.bitwise_xor(a_labels[:, None], virt_irrep[None, :])[None, :, :]
        == pair_labels[:, None, None]
    )
    return mirrored * kept_mask.astype(jnp.float32)


def solution(mesh):
    in_specs = (P("row", None, "col"), P(None, "col", "row", None), P(), P(), P())
    out_specs = P("col", "row", None)
    return jax.shard_map(local, mesh=mesh, in_specs=in_specs, out_specs=out_specs, check_vma=False)
```

profile of v0, /device:TPU:0, one launch (start us, length us, event | category | flops | bytes accessed | tf_op | source)
XLA Modules:
  0.0 375.9 jit_solution(2555133089651261318)
XLA Ops:
  6.5 0.0 reduce-scatter.2.cloned.1.call-start
  6.5 0.7 slice.3
  7.2 0.8 dynamic_slice.11
  8.0 0.9 fusion.6
  8.9 0.1 broadcast_xor_fusion.1
  8.9 0.2 fusion.4
  9.1 32.6 %all_gather.3 = f32[64,2,160]{2,1,0:T(2,128)S(1)} all-gather(f32[8,2,160]{2,1,0:T(2,128)} %param.5), channel_id=1, replica_groups=mesh['row'=8,'col'=4] {'row'}, dimensions={0}, use_global_device_ids=true | all-gather | bytes 92160 | tf_op jit(solution)/shard_map/all_gather | solution.py:46
  41.7 0.8 compare_select_fusion
  42.5 0.1 reshape.68
  42.7 79.4 %fusion = f32[64,80,640]{2,0,1:T(8,128)} fusion(f32[64,320,1]{1,0,2:T(8,128)S(1)} %reshape.68, f32[40,8,80,640]{3,2,1,0:T(8,128)} %bitcast.26), kind=kOutput, calls=%fused_computation | convolution fusion | flops 12582912000 | bytes 78725120 | tf_op jit(solution)/shard_map/dot_general | solution.py:51
  122.1 0.0 reduce-scatter.2.cloned.1.call-update
  122.2 101.4 %reduce-scatter.2.cloned.1.call-done = f32[16,80,640]{2,0,1:T(8,128)} async-done(((f32[64,80,640]{2,0,1:T(8,128)}), f32[16,80,640]{2,0,1:T(8,128)}) %reduce-scatter.2.cloned.1.call-update) | async-done | bytes 3276816 | tf_op jit(solution)/shard_map/reduce_scatter | solution.py:8
  223.6 5.6 %copy.16 = f32[16,80,640]{1,0,2:T(8,128)} copy(f32[16,80,640]{2,0,1:T(8,128)} %reduce-scatter.2.cloned.1.call-done) | data formatting | bytes 6553600 | tf_op jit(solution)/shard_map/reduce_scatter | solution.py:8
  229.2 5.6 %all-to-all-start = ((f32[16,80,640]{1,0,2:T(8,128)}), f32[16,80,640]{1,0,2:T(8,128)}, u32[]{:S(2)}, u32[]{:S(2)}) async-start(f32[16,80,640]{1,0,2:T(8,128)} %copy.16), calls=%async_computation.1 | async-start | bytes 10485760 | tf_op jit(solution)/shard_map/all_to_all | solution.py:12
  234.8 0.0 copy-done.2
  234.9 0.1 dynamic_slice.10
  234.9 0.0 copy-done.1
  234.9 0.1 dynamic_slice.9
  235.0 0.1 broadcast_xor_fusion
  235.1 115.3 %all-to-all-done = f32[16,80,640]{1,0,2:T(8,128)} async-done(((f32[16,80,640]{1,0,2:T(8,128)}), f32[16,80,640]{1,0,2:T(8,128)}, u32[]{:S(2)}, u32[]{:S(2)}) %all-to-all-start) | async-done | bytes 3276832 | tf_op jit(solution)/shard_map/all_to_all | solution.py:12
  350.4 7.9 %copy.29 = f32[16,80,8,80]{1,2,0,3:T(8,128)} copy(f32[16,80,8,80]{1,0,3,2:T(8,128)} %bitcast.1) | data formatting | bytes 6553600 | tf_op jit(solution)/shard_map/all_to_all | solution.py:12
  358.3 5.5 %all_to_all.16 = f32[16,640,80]{1,0,2:T(8,128)} reshape(f32[16,8,80,80]{2,1,0,3:T(8,128)} %bitcast.27) | data formatting | bytes 6553600 | tf_op jit(solution)/shard_map/all_to_all | solution.py:12
  363.8 2.5 fusion.3
  366.4 2.7 copy.18
  (4 shorter events, 0.0 us)
Async XLA Ops:
  6.5 217.0 %reduce-scatter.2.cloned.1.call-start = ((), (), s32[]{:S(2)}) async-start(), calls=%async_computation.2 | async-start | bytes 16384000 | tf_op jit(solution)/shard_map/reduce_scatter | solution.py:8
  229.2 5.6 %copy-start.2 = (s32[64]{0:T(128)S(1)}, s32[64]{0:T(128)}, u32[]{:S(2)}) copy-start(s32[64]{0:T(128)} %param.8) | copy-start | bytes 772
  229.2 5.7 %copy-start.1 = (s32[640]{0:T(1024)S(1)}, s32[640]{0:T(1024)}, u32[]{:S(2)}) copy-start(s32[640]{0:T(1024)} %param.7) | copy-start | bytes 7684
  229.2 121.2 %all-to-all-start = ((f32[16,80,640]{1,0,2:T(8,128)}), f32[16,80,640]{1,0,2:T(8,128)}, u32[]{:S(2)}, u32[]{:S(2)}) async-start(f32[16,80,640]{1,0,2:T(8,128)} %copy.16), calls=%async_computation.1 | async-start | bytes 10485760 | tf_op jit(solution)/shard_map/all_to_all | solution.py:12
  358.3 5.5 %copy-start = (f32[16,80,640]{2,0,1:T(8,128)S(1)}, f32[16,80,640]{2,0,1:T(8,128)}, u32[]{:S(2)}) copy-start(f32[16,80,640]{2,0,1:T(8,128)} %reduce-scatter.2.cloned.1.call-done) | copy-start | bytes 9830404
Sparse Core Ops, SparseCore 0:
  122.3 101.2 reduce-scatter.1
where the time goes:
time: 376 us
  waiting for transfers between devices  217 us (58%)
  matrix products  80.5 us (21%)
  blocking collectives  32.6 us (9%)
  local copies, waits for them, and re-layouts  23.5 us (6%)
  between operations  13.4 us (4%)
  starting transfers between devices  5.64 us (2%)
    all_to_all x1, waiting for transfers between devices, mirror_after(): lax.all_to_all(owned, 'row', split_axis=2, concat_axis=1, tiled=True)  115 us
    reduce_scatter x1, waiting for transfers between devices, reduce_pairs(): lax.psum_scatter(partial_sums, 'col', scatter_dimension=0, tiled=True)  101 us
    dot_general x1, matrix products, local(): jnp.dot(masked.reshape(pair_count, slab_width * d_width), integrals.resha...  79.4 us
    all_gather x1, blocking collectives, local(): gathered = lax.all_gather(amplitudes, 'row', axis=0, tiled=True)  32.6 us
    all_to_all x2, local copies, waits for them, and re-layouts, mirror_after(): lax.all_to_all(owned, 'row', split_axis=2, concat_axis=1, tiled=True)  13.4 us
  transfers between devices with their start and end apart: 2, of which 2 were waited for; matrix products, arithmetic and copies ran while one was open for 0% of the time, Pallas kernels for 0%

commit v1 on v0

--- a/solution.py
+++ b/solution.py
@@ -43,7 +43,9 @@
     full_width = integrals.shape[3]
     row_index = lax.axis_index("row")
     col_index = lax.axis_index("col")
-    gathered = lax.all_gather(amplitudes, "row", axis=0, tiled=True)
+    gathered = jnp.concatenate(
+        lax.all_to_all(jnp.stack([amplitudes] * lax.axis_size("row")), "row", 0, 0), axis=0
+    )
     pair_count = gathered.shape[0]
     c_labels = virt_irrep[:slab_width]
     d_labels = lax.dynamic_slice_in_dim(virt_irrep, col_index * d_width, d_width)

time: 376 us -> 354 us (0.941)
  blocking collectives: 32.6 us -> 0 us
  starting transfers between devices: 5.64 us -> 13 us
    all_gather x1 -> x0, blocking collectives: 32.6 us -> none  [local(): gathered = lax.all_gather(amplitudes, 'row', axis=0, tiled=True)]
    all_to_all x0 -> x1, starting transfers between devices: none -> 7.31 us  [local(): lax.all_to_all(jnp.stack([amplitudes] * lax.axis_size('row')), 'row', 0, 0)]
    all_to_all x0 -> x1, waiting for transfers between devices: none -> 3.96 us  [local(): lax.all_to_all(jnp.stack([amplitudes] * lax.axis_size('row')), 'row', 0, 0)]
  transfers between devices with their start and end apart: 2 -> 3, of which waited for: 2 -> 3; matrix products, arithmetic and copies ran while one was open for 0% -> 1% of each run, Pallas kernels for 0% -> 0%
where the time goes in v1:
time: 354 us; the launch traced here: 353 us
  waiting for transfers between devices  218 us (62%)
  matrix products  80.6 us (23%)
  local copies, waits for them, and re-layouts  25.6 us (7%)
  between operations  13.4 us (4%)
  starting transfers between devices  13 us (4%)
    all_to_all x1, waiting for transfers between devices, mirror_after(): lax.all_to_all(owned, 'row', split_axis=2, concat_axis=1, tiled=True)  115 us
    reduce_scatter x1, waiting for transfers between devices, reduce_pairs(): lax.psum_scatter(partial_sums, 'col', scatter_dimension=0, tiled=True)  98.3 us
    dot_general x1, matrix products, local(): jnp.dot(masked.reshape(pair_count, slab_width * d_width), integrals.resha...  79.5 us
    all_to_all x2, local copies, waits for them, and re-layouts, mirror_after(): lax.all_to_all(owned, 'row', split_axis=2, concat_axis=1, tiled=True)  13.4 us
    all_to_all x1, starting transfers between devices, local(): lax.all_to_all(jnp.stack([amplitudes] * lax.axis_size('row')), 'row', 0, 0)  7.31 us
  transfers between devices with their start and end apart: 3, of which 3 were waited for; matrix products, arithmetic and copies ran while one was open for 1% of the time, Pallas kernels for 0%

profile of v1, /device:TPU:0, one launch (start us, length us, event | category | flops | bytes accessed | tf_op | source)
XLA Modules:
  0.0 353.1 jit_solution(2218227761767054255)
XLA Ops:
  6.5 1.4 stack.2
  7.9 7.3 %all-to-all-start = ((f32[8,8,2,160]{3,2,1,0:T(2,128)}), f32[8,8,2,160]{3,2,1,0:T(2,128)S(1)}, u32[]{:S(2)}, u32[]{:S(2)}) async-start(f32[8,8,2,160]{3,2,1,0:T(2,128)} %stack.2), calls=%async_computation | async-start | bytes 262144 | tf_op jit(solution)/shard_map/all_to_all | solution.py:47
  15.3 0.0 reduce-scatter.2.cloned.1.call-start
  15.3 0.7 slice.3
  16.0 0.8 dynamic_slice.11
  16.8 0.7 eq.60
  17.5 0.9 fusion.6
  18.4 0.2 fusion.4
  18.6 0.1 broadcast_xor_fusion.1
  18.6 4.0 %all-to-all-done = f32[8,8,2,160]{3,2,1,0:T(2,128)S(1)} async-done(((f32[8,8,2,160]{3,2,1,0:T(2,128)}), f32[8,8,2,160]{3,2,1,0:T(2,128)S(1)}, u32[]{:S(2)}, u32[]{:S(2)}) %all-to-all-start) | async-done | bytes 81952 | tf_op jit(solution)/shard_map/all_to_all | solution.py:47
  22.6 0.1 compare_select_fusion
  22.7 0.1 reshape.89
  22.9 79.5 %fusion = f32[64,80,640]{2,0,1:T(8,128)} fusion(f32[64,320,1]{1,0,2:T(8,128)S(1)} %reshape.89, f32[40,8,80,640]{3,2,1,0:T(8,128)} %bitcast.26), kind=kOutput, calls=%fused_computation | convolution fusion | flops 12582912000 | bytes 78725120 | tf_op jit(solution)/shard_map/dot_general | solution.py:53
  102.4 98.3 %reduce-scatter.2.cloned.1.call-done = f32[16,80,640]{2,0,1:T(8,128)} async-done(((f32[64,80,640]{2,0,1:T(8,128)}), f32[16,80,640]{2,0,1:T(8,128)}) %reduce-scatter.2.cloned.1.call-update) | async-done | bytes 3276816 | tf_op jit(solution)/shard_map/reduce_scatter | solution.py:8
  200.8 5.6 %copy.16 = f32[16,80,640]{1,0,2:T(8,128)} copy(f32[16,80,640]{2,0,1:T(8,128)} %reduce-scatter.2.cloned.1.call-done) | data formatting | bytes 6553600 | tf_op jit(solution)/shard_map/reduce_scatter | solution.py:8
  206.4 5.6 %all-to-all-start.1 = ((f32[16,80,640]{1,0,2:T(8,128)}), f32[16,80,640]{1,0,2:T(8,128)}, u32[]{:S(2)}, u32[]{:S(2)}) async-start(f32[16,80,640]{1,0,2:T(8,128)} %copy.16), calls=%async_computation.2 | async-start | bytes 10485760 | tf_op jit(solution)/shard_map/all_to_all | solution.py:12
  212.1 0.1 dynamic_slice.10
  212.1 0.1 dynamic_slice.9
  212.2 0.1 broadcast_xor_fusion
  212.3 115.3 %all-to-all-done.1 = f32[16,80,640]{1,0,2:T(8,128)} async-done(((f32[16,80,640]{1,0,2:T(8,128)}), f32[16,80,640]{1,0,2:T(8,128)}, u32[]{:S(2)}, u32[]{:S(2)}) %all-to-all-start.1) | async-done | bytes 3276832 | tf_op jit(solution)/shard_map/all_to_all | solution.py:12
  327.7 7.8 %copy.29 = f32[16,80,8,80]{1,2,0,3:T(8,128)} copy(f32[16,80,8,80]{1,0,3,2:T(8,128)} %bitcast.1) | data formatting | bytes 6553600 | tf_op jit(solution)/shard_map/all_to_all | solution.py:12
  335.5 5.5 %all_to_all.20 = f32[16,640,80]{1,0,2:T(8,128)} reshape(f32[16,8,80,80]{2,1,0,3:T(8,128)} %bitcast.27) | data formatting | bytes 6553600 | tf_op jit(solution)/shard_map/all_to_all | solution.py:12
  341.0 2.5 fusion.3
  343.6 2.7 copy.18
  (7 shorter events, 0.0 us)
Async XLA Ops:
  7.9 14.7 %all-to-all-start = ((f32[8,8,2,160]{3,2,1,0:T(2,128)}), f32[8,8,2,160]{3,2,1,0:T(2,128)S(1)}, u32[]{:S(2)}, u32[]{:S(2)}) async-start(f32[8,8,2,160]{3,2,1,0:T(2,128)} %stack.2), calls=%async_computation | async-start | bytes 262144 | tf_op jit(solution)/shard_map/all_to_all | solution.py:47
  15.3 185.5 %reduce-scatter.2.cloned.1.call-start = ((), (), s32[]{:S(2)}) async-start(), calls=%async_computation.3 | async-start | bytes 16384000 | tf_op jit(solution)/shard_map/reduce_scatter | solution.py:8
  206.4 5.7 %copy-start.2 = (s32[64]{0:T(128)S(1)}, s32[64]{0:T(128)}, u32[]{:S(2)}) copy-start(s32[64]{0:T(128)} %param.8) | copy-start | bytes 772
  206.4 5.7 %copy-start.1 = (s32[640]{0:T(1024)S(1)}, s32[640]{0:T(1024)}, u32[]{:S(2)}) copy-start(s32[640]{0:T(1024)} %param.7) | copy-start | bytes 7684
  206.4 121.2 %all-to-all-start.1 = ((f32[16,80,640]{1,0,2:T(8,128)}), f32[16,80,640]{1,0,2:T(8,128)}, u32[]{:S(2)}, u32[]{:S(2)}) async-start(f32[16,80,640]{1,0,2:T(8,128)} %copy.16), calls=%async_computation.2 | async-start | bytes 10485760 | tf_op jit(solution)/shard_map/all_to_all | solution.py:12
  335.5 5.5 %copy-start = (f32[16,80,640]{2,0,1:T(8,128)S(1)}, f32[16,80,640]{2,0,1:T(8,128)}, u32[]{:S(2)}) copy-start(f32[16,80,640]{2,0,1:T(8,128)} %reduce-scatter.2.cloned.1.call-done) | copy-start | bytes 9830404
Sparse Core Ops, SparseCore 0:
  102.6 98.1 reduce-scatter.1
